TPU v7x, 32 devices: a whole 2x2x4 slice. The times are simulated.
32 devices in a mesh: dp: 4 (over z), row: 2 (over x), col: 4 (over y, core).
Axes of the slice: x: 2, y: 2, z: 4, core: 2. Of those that a mesh axis runs over, the one named last changes fastest.
Arguments:
- tokens: bfloat16 [768, 16384], P('row', ('dp', 'col')), may hold values from -6 to 6
- ln_gain: float32 [768], P('row'), may hold values from 0.5 to 1.5
- ln_bias: float32 [768], P('row'), may hold values from -0.3 to 0.3
- qkv_weight: bfloat16 [768, 3, 768], P('row', None, 'col'), may hold values from -0.21875 to 0.21875
- out_weight: bfloat16 [768, 768], P('col', 'row'), may hold values from -6 to 6
- up_weight: bfloat16 [768, 3072], P('row', 'col'), may hold values from -0.21875 to 0.21875
- down_weight: bfloat16 [768, 3072], P('row', 'col'), may hold values from -0.21875 to 0.21875
- mod_weight: bfloat16 [3, 768, 768], P(None, 'row'), may hold values from -0.109375 to 0.109375
- timestep: int32 [8], replicated, may hold values from 0 to 999
- block_size: int32 [8], replicated, may hold values from 32 to 256, as said below
- cotangent: bfloat16 [768, 16384], P('row', ('dp', 'col')), may hold values from -6 to 6
Outputs:
- output: bfloat16 [768, 16384], P('row', ('dp', 'col'))
- tokens_grad: float32 [768, 16384], P('row', ('dp', 'col'))
- ln_gain_grad: float32 [768], P('row')
- ln_bias_grad: float32 [768], P('row')
- qkv_grad: float32 [768, 3, 768], P('row', None, 'col')
- out_grad: float32 [768, 768], P('col', 'row')
- up_grad: float32 [768, 3072], P('row', 'col')
- down_grad: float32 [768, 3072], P('row', 'col')
- mod_grad: float32 [3, 768, 768], P(None, 'row')
Inputs may be any that keep to these rules, and one draw needn't show every extreme that they name: `block_size`: each entry is 256 halved zero to three times; some sequence has 256.
All inputs are finite; a program needn't handle non-finite values.
Results may differ from a plain program's by a relative error of at most 0.02.
Values may be sent and summed in bfloat16 or wider, within the bound.
No kernel may reach another device: no remote copies, remote signals or barrier semaphores. Data moves between devices by JAX's collectives and lax.ppermute only.
A program may use at most 256 MiB of HBM per device.

v0:
```python
from functools import partial
import math
import jax
import jax.numpy as jnp
from jax import lax
from jax.sharding import PartitionSpec as P

HEAD_DIM = 64
LENGTH = 2048
EPSILON = 1e-05
HIGH = lax.Precision.HIGHEST


def time_embed(steps_in, width_all):
    half_width = width_all // 2
    frequency = jnp.exp(-math.log(10000.0) * jnp.arange(half_width, dtype=jnp.float32) / half_width)
    angles = steps_in.astype(jnp.float32)[:, None] * frequency[None, :]
    return jnp.concatenate([jnp.sin(angles), jnp.cos(angles)], axis=1)


def rope_tables(length, head_width):
    half_dim = head_width // 2
    frequency = jnp.exp(-math.log(10000.0) * jnp.arange(half_dim, dtype=jnp.float32) / half_dim)
    angles = jnp.arange(length, dtype=jnp.float32)[:, None] * frequency[None, :]
    return (jnp.cos(angles), jnp.sin(angles))


def rotate(vector, cosine, sine_tab):
    half_dim = vector.shape[-1] // 2
    front_half, back_half = (vector[..., :half_dim], vector[..., half_dim:])
    return jnp.concatenate(
        [front_half * cosine - back_half * sine_tab, back_half * cosine + front_half * sine_tab],
        axis=-1,
    )


def unrotate(grads_in, cosine, sine_tab):
    half_dim = grads_in.shape[-1] // 2
    front_half, back_half = (grads_in[..., :half_dim], grads_in[..., half_dim:])
    return jnp.concatenate(
        [front_half * cosine + back_half * sine_tab, back_half * cosine - front_half * sine_tab],
        axis=-1,
    )


def token_totals(first_terms, second_terms):
    return lax.psum((jnp.sum(first_terms, axis=1), jnp.sum(second_terms, axis=1)), "row")


def norm_forward(values, width_all):
    sum_plain, sum_square = token_totals(values, values * values)
    mean_row = sum_plain / width_all
    inv_std = lax.rsqrt(sum_square / width_all - mean_row * mean_row + EPSILON)
    return ((values - mean_row[:, None]) * inv_std[:, None], inv_std)


def norm_backward(grad_norm, normed, inv_std, width_all):
    sum_plain, sum_cross = token_totals(grad_norm, grad_norm * normed)
    return inv_std[:, None] * (
        grad_norm - sum_plain[:, None] / width_all - normed * (sum_cross[:, None] / width_all)
    )


def gather_col(local_part):
    return lax.all_gather(local_part, "col", axis=0, tiled=True)


def gather_rows(local_part):
    return lax.all_gather(local_part, "row", axis=0, tiled=True)


def row_product(gathered, tile_part):
    return lax.psum_scatter(
        jnp.dot(gathered, tile_part, preferred_element_type=jnp.float32),
        "row",
        scatter_dimension=0,
        tiled=True,
    )


def col_product(gathered, tile_part):
    return lax.psum_scatter(
        jnp.dot(gathered, tile_part, preferred_element_type=jnp.float32),
        "col",
        scatter_dimension=0,
        tiled=True,
    )


def block_index(block_lens, length):
    positions = jnp.arange(length, dtype=jnp.int32)
    return positions[None, :] // block_lens[:, None]


def masked_scores(query_part, key_rows, key_block, query_block, score_scale):
    scores = (
        jnp.einsum("sqhd,skhd->shqk", query_part, key_rows, preferred_element_type=jnp.float32)
        * score_scale
    )
    visible = key_block[:, None, None, :] <= query_block[:, None, :, None]
    return jnp.where(visible, scores, -1e30)


def attend_forward(queries, key_rows, value_rows, block_lens):
    length = queries.shape[1]
    rows_per = min(512, length)
    score_scale = queries.shape[3] ** (-0.5)
    key_block = block_index(block_lens, length)

    def one_block(offset):
        query_part = lax.dynamic_slice_in_dim(queries, offset, rows_per, 1)
        query_block = lax.dynamic_slice_in_dim(key_block, offset, rows_per, 1)
        scores = masked_scores(query_part, key_rows, key_block, query_block, score_scale)
        row_top = jnp.max(scores, axis=-1, keepdims=True)
        raised = jnp.exp(scores - row_top)
        row_total = jnp.sum(raised, axis=-1, keepdims=True)
        weights = (raised / row_total).astype(jnp.bfloat16)
        block_out = jnp.einsum(
            "shqk,skhd->sqhd", weights, value_rows, preferred_element_type=jnp.float32
        )
        return (block_out, row_top[..., 0] + jnp.log(row_total[..., 0]))

    offsets = jnp.arange(0, length, rows_per, dtype=jnp.int32)
    block_outs, log_totals = lax.map(one_block, offsets)
    return (jnp.moveaxis(block_outs, 0, 1).reshape(queries.shape), log_totals)


def attend_backward(queries, key_rows, value_rows, grad_mixed, log_totals, block_lens):
    length = queries.shape[1]
    rows_per = min(512, length)
    score_scale = queries.shape[3] ** (-0.5)
    key_block = block_index(block_lens, length)

    def one_block(running, element):
        grad_keys, grad_values = running
        offset, log_part = element
        query_part = lax.dynamic_slice_in_dim(queries, offset, rows_per, 1)
        grad_part = lax.dynamic_slice_in_dim(grad_mixed, offset, rows_per, 1)
        query_block = lax.dynamic_slice_in_dim(key_block, offset, rows_per, 1)
        scores = masked_scores(query_part, key_rows, key_block, query_block, score_scale)
        weights = jnp.exp(scores - log_part[..., None])
        grad_weights = jnp.einsum(
            "sqhd,skhd->shqk", grad_part, value_rows, preferred_element_type=jnp.float32
        )
        grad_scores = weights * (
            grad_weights - jnp.sum(weights * grad_weights, axis=-1, keepdims=True)
        )
        grad_scores = grad_scores.astype(jnp.bfloat16)
        grad_query = (
            jnp.einsum("shqk,skhd->sqhd", grad_scores, key_rows, preferred_element_type=jnp.float32)
            * score_scale
        )
        grad_keys = (
            grad_keys
            + jnp.einsum(
                "shqk,sqhd->skhd", grad_scores, query_part, preferred_element_type=jnp.float32
            )
            * score_scale
        )
        grad_values = grad_values + jnp.einsum(
            "shqk,sqhd->skhd",
            weights.astype(jnp.bfloat16),
            grad_part,
            preferred_element_type=jnp.float32,
        )
        return ((grad_keys, grad_values), grad_query)

    offsets = jnp.arange(0, length, rows_per, dtype=jnp.int32)
    zero_grads = jnp.zeros(queries.shape, jnp.float32)
    (grad_keys, grad_values), grad_queries = lax.scan(
        one_block, (zero_grads, zero_grads), (offsets, log_totals)
    )
    return (jnp.moveaxis(grad_queries, 0, 1).reshape(queries.shape), grad_keys, grad_values)


def local(
    tokens,
    ln_gain,
    ln_bias,
    qkv_weight,
    out_weight,
    up_weight,
    down_weight,
    mod_weight,
    timestep,
    block_size,
    cotangent,
):
    n_row = lax.axis_size("row")
    n_col = lax.axis_size("col")
    width_all = mod_weight.shape[2]
    feat_local, local_tokens = tokens.shape
    group_tokens = local_tokens * n_col
    seq_here = group_tokens // n_row // LENGTH
    heads_here = qkv_weight.shape[2] // HEAD_DIM
    group_index = lax.axis_index("dp")
    first_token = group_index * group_tokens + lax.axis_index("col") * local_tokens
    seq_count = max(1, local_tokens // LENGTH)
    token_span = local_tokens // seq_count
    steps_here = lax.dynamic_slice_in_dim(timestep, first_token // LENGTH, seq_count, 0)
    embedded = time_embed(steps_here, width_all)
    modulation = jnp.einsum("nd,ked->kne", embedded, mod_weight.astype(jnp.float32), precision=HIGH)

    def per_token(table):
        return jnp.broadcast_to(table[:, None, :], (seq_count, token_span, feat_local)).reshape(
            local_tokens, feat_local
        )

    def per_sequence(values):
        return jnp.sum(values.reshape(seq_count, token_span, feat_local), axis=1)

    scale_tok = per_token(modulation[0])
    shift_tok = per_token(modulation[1])
    gate_tok = per_token(modulation[2])
    resid = tokens.astype(jnp.float32).T
    norm_one, inv_one = norm_forward(resid, width_all)
    act_one = (norm_one * ln_gain + ln_bias).astype(jnp.bfloat16)
    act_one_all = gather_col(act_one)
    qkv_tile = qkv_weight.reshape(feat_local, -1)
    projected = row_product(act_one_all, qkv_tile).reshape(
        seq_here, LENGTH, 3, heads_here, HEAD_DIM
    )
    cosine, sine_tab = rope_tables(LENGTH, HEAD_DIM)
    cosine = cosine[None, :, None, :]
    sine_tab = sine_tab[None, :, None, :]
    queries = rotate(projected[:, :, 0], cosine, sine_tab).astype(jnp.bfloat16)
    key_rows = rotate(projected[:, :, 1], cosine, sine_tab).astype(jnp.bfloat16)
    value_rows = projected[:, :, 2].astype(jnp.bfloat16)
    seq_first = (group_index * n_row + lax.axis_index("row")) * seq_here
    block_lens = lax.dynamic_slice_in_dim(block_size, seq_first, seq_here, 0)
    attended, log_totals = attend_forward(queries, key_rows, value_rows, block_lens)
    attn_mix = attended.reshape(seq_here * LENGTH, heads_here * HEAD_DIM).astype(jnp.bfloat16)
    attn_mix_all = gather_rows(attn_mix)
    branch_one = col_product(attn_mix_all, out_weight)
    hidden_one = resid + branch_one
    norm_two, inv_two = norm_forward(hidden_one, width_all)
    act_two = (norm_two * (1.0 + scale_tok) + shift_tok).astype(jnp.bfloat16)
    act_two_all = gather_col(act_two)
    pre_act = row_product(act_two_all, up_weight)
    gelu_out = jax.nn.gelu(pre_act, approximate=True).astype(jnp.bfloat16)
    gelu_all = gather_rows(gelu_out)
    branch_two = col_product(gelu_all, down_weight.T)
    result = hidden_one + (1.0 + gate_tok) * branch_two
    grad_out = cotangent.astype(jnp.float32).T
    gate_term = grad_out * branch_two
    grad_two = (grad_out * (1.0 + gate_tok)).astype(jnp.bfloat16)
    grad_two_all = gather_col(grad_two)
    grad_gelu = row_product(grad_two_all, down_weight)
    down_grad = jnp.einsum("td,tf->df", grad_two_all, gelu_all, preferred_element_type=jnp.float32)
    _, gelu_pull = jax.vjp(partial(jax.nn.gelu, approximate=True), pre_act)
    grad_pre = gelu_pull(grad_gelu)[0].astype(jnp.bfloat16)
    grad_pre_all = gather_rows(grad_pre)
    grad_act_two = col_product(grad_pre_all, up_weight.T)
    up_grad = jnp.einsum("td,tf->df", act_two_all, grad_pre_all, preferred_element_type=jnp.float32)
    scale_term = grad_act_two * norm_two
    grad_hidden = grad_out + norm_backward(
        grad_act_two * (1.0 + scale_tok), norm_two, inv_two, width_all
    )
    grad_one = grad_hidden.astype(jnp.bfloat16)
    grad_one_all = gather_col(grad_one)
    grad_attn = row_product(grad_one_all, out_weight.T)
    out_grad = jnp.einsum(
        "tc,td->cd", attn_mix_all, grad_one_all, preferred_element_type=jnp.float32
    )
    grad_attn = grad_attn.astype(jnp.bfloat16).reshape(seq_here, LENGTH, heads_here, HEAD_DIM)
    grad_queries, grad_keys, grad_values = attend_backward(
        queries, key_rows, value_rows, grad_attn, log_totals, block_lens
    )
    grad_queries = unrotate(grad_queries, cosine, sine_tab)
    grad_keys = unrotate(grad_keys, cosine, sine_tab)
    grad_projected = jnp.stack([grad_queries, grad_keys, grad_values], axis=2).astype(jnp.bfloat16)
    grad_projected = grad_projected.reshape(seq_here * LENGTH, 3 * heads_here * HEAD_DIM)
    grad_proj_all = gather_rows(grad_projected)
    grad_act_one = col_product(grad_proj_all, qkv_tile.T)
    qkv_grad = jnp.einsum(
        "td,tk->dk", act_one_all, grad_proj_all, preferred_element_type=jnp.float32
    ).reshape(qkv_weight.shape)
    gain_part = jnp.sum(grad_act_one * norm_one, axis=0)
    bias_part = jnp.sum(grad_act_one, axis=0)
    tokens_grad = grad_hidden + norm_backward(grad_act_one * ln_gain, norm_one, inv_one, width_all)
    grad_mod = jnp.stack(
        [per_sequence(scale_term), per_sequence(grad_act_two), per_sequence(gate_term)]
    )
    mod_part = jnp.einsum("nd,kne->ked", embedded, grad_mod, precision=HIGH)
    gain_grad, bias_grad, mod_grad = (
        lax.psum(gain_part.astype(jnp.bfloat16), ("dp", "col")).astype(jnp.float32),
        lax.psum(bias_part.astype(jnp.bfloat16), ("dp", "col")).astype(jnp.float32),
        lax.psum(mod_part.astype(jnp.bfloat16), ("dp", "col")).astype(jnp.float32),
    )
    qkv_grad, out_grad, up_grad, down_grad = (
        lax.psum(qkv_grad.astype(jnp.bfloat16), "dp").astype(jnp.float32),
        lax.psum(out_grad.astype(jnp.bfloat16), "dp").astype(jnp.float32),
        lax.psum(up_grad.astype(jnp.bfloat16), "dp").astype(jnp.float32),
        lax.psum(down_grad.astype(jnp.bfloat16), "dp").astype(jnp.float32),
    )
    return (
        result.astype(jnp.bfloat16).T,
        tokens_grad.T,
        gain_grad,
        bias_grad,
        qkv_grad,
        out_grad,
        up_grad,
        down_grad,
        mod_grad,
    )


def solution(mesh):
    placed = (
        P("row", ("dp", "col")),
        P("row"),
        P("row"),
        P("row", None, "col"),
        P("col", "row"),
        P("row", "col"),
        P("row", "col"),
        P(None, "row", None),
        P(),
        P(),
        P("row", ("dp", "col")),
    )
    return jax.shard_map(
        local,
        mesh=mesh,
        in_specs=placed,
        out_specs=(
            P("row", ("dp", "col")),
            P("row", ("dp", "col")),
            P("row"),
            P("row"),
            P("row", None, "col"),
            P("col", "row"),
            P("row", "col"),
            P("row", "col"),
            P(None, "row", None),
        ),
        check_vma=False,
    )
```

profile of v0, /device:TPU:0, one launch (start us, length us, event | category | flops | bytes accessed | tf_op | source)
XLA Modules:
  0.0 1632.1 jit_solution(8770067134209926731)
XLA Ops:
  17.3 30.4 %all-gather.9.cloned.1.call-done = bf16[4096,384]{1,0:T(8,128)(2,1)} async-done(((bf16[1024,384]{1,0:T(8,128)(2,1)}), bf16[4096,384]{1,0:T(8,128)(2,1)}) %all-gather.9.cloned.1.call-update) | async-done | bytes 3145744 | tf_op jit(solution)/shard_map/all_gather | solution.py:65
  58.9 106.6 %reduce-scatter.9.cloned.1.call-done = f32[2048,576]{0,1:T(8,128)} async-done(((f32[4096,576]{0,1:T(8,128)}), f32[2048,576]{0,1:T(8,128)}) %reduce-scatter.9.cloned.1.call-update) | async-done | bytes 4718608 | tf_op jit(solution)/shard_map/reduce_scatter | solution.py:73
  170.5 98.7 %while.27 = (s32[]{:T(128)}, bf16[4,1,512,3,64]{2,4,3,1,0:T(8,128)(2,1)}, f32[4,1,3,512]{3,2,1,0:T(4,128)S(1)}, s32[1,2048]{1,0:T(1,128)S(1)}, s32[4]{0:T(128)S(...) while((s32[]{:T(128)}, ...), condition=%wide.region_8.10_spmd, body=%wide.region_5.9_spmd.sunk | while | flops 844102144 | bytes 50471144 | solution.py:124
  272.4 27.1 %all-gather.11.cloned.1.call-done = bf16[4096,192]{0,1:T(8,128)(2,1)} async-done(((bf16[2048,192]{0,1:T(8,128)(2,1)}), bf16[4096,192]{0,1:T(8,128)(2,1)}) %all-gather.11.cloned.1.call-update) | async-done | bytes 1572880 | tf_op jit(solution)/shard_map/all_gather | solution.py:69
  311.7 52.2 %reduce-scatter.11.cloned.1.call-done = f32[1024,384]{1,0:T(8,128)} async-done(((f32[4096,384]{1,0:T(8,128)}), f32[1024,384]{1,0:T(8,128)}) %reduce-scatter.11.cloned.1.call-update) | async-done | bytes 1572880 | tf_op jit(solution)/shard_map/reduce_scatter | solution.py:82
  374.6 19.8 %all-gather.17.cloned.1.call-done = bf16[4096,384]{1,0:T(8,128)(2,1)} async-done(((bf16[1024,384]{1,0:T(8,128)(2,1)}), bf16[4096,384]{1,0:T(8,128)(2,1)}) %all-gather.17.cloned.1.call-update) | async-done | bytes 3145744 | tf_op jit(solution)/shard_map/all_gather | solution.py:65
  394.4 10.4 fusion.89
  404.9 20.0 %all-gather.13.cloned.1.call-done = bf16[4096,384]{1,0:T(8,128)(2,1)} async-done(((bf16[1024,384]{1,0:T(8,128)(2,1)}), bf16[4096,384]{1,0:T(8,128)(2,1)}) %all-gather.13.cloned.1.call-update) | async-done | bytes 3145744 | tf_op jit(solution)/shard_map/all_gather | solution.py:65
  425.0 10.5 fusion.87
  436.0 135.8 %reduce-scatter.17.cloned.1.call-done = f32[2048,768]{1,0:T(8,128)} async-done(((f32[4096,768]{1,0:T(8,128)}), f32[2048,768]{1,0:T(8,128)}) %reduce-scatter.17.cloned.1.call-update) | async-done | bytes 6291472 | tf_op jit(solution)/shard_map/reduce_scatter | solution.py:73
  571.8 146.9 %reduce-scatter.13.cloned.1.call-done = f32[2048,768]{1,0:T(8,128)} async-done(((f32[4096,768]{1,0:T(8,128)}), f32[2048,768]{1,0:T(8,128)}) %reduce-scatter.13.cloned.1.call-update) | async-done | bytes 6291472 | tf_op jit(solution)/shard_map/reduce_scatter | solution.py:73
  728.4 79.9 %all-gather.19.cloned.1.call-done = bf16[4096,768]{1,0:T(8,128)(2,1)} async-done(((bf16[2048,768]{1,0:T(8,128)(2,1)}), bf16[4096,768]{1,0:T(8,128)(2,1)}) %all-gather.19.cloned.1.call-update) | async-done | bytes 6291472 | tf_op jit(solution)/shard_map/all_gather | solution.py:69
  808.3 9.4 fusion.90
  817.7 72.3 %all-gather.15.cloned.1.call-done = bf16[4096,768]{1,0:T(8,128)(2,1)} async-done(((bf16[2048,768]{1,0:T(8,128)(2,1)}), bf16[4096,768]{1,0:T(8,128)(2,1)}) %all-gather.15.cloned.1.call-update) | async-done | bytes 6291472 | tf_op jit(solution)/shard_map/all_gather | solution.py:69
  899.5 52.0 %reduce-scatter.19.cloned.1.call-done = f32[1024,384]{1,0:T(8,128)} async-done(((f32[4096,384]{1,0:T(8,128)}), f32[1024,384]{1,0:T(8,128)}) %reduce-scatter.19.cloned.1.call-update) | async-done | bytes 1572880 | tf_op jit(solution)/shard_map/reduce_scatter | solution.py:82
  959.2 53.5 %reduce-scatter.15.cloned.1.call-done = f32[1024,384]{1,0:T(8,128)} async-done(((f32[4096,384]{1,0:T(8,128)}), f32[1024,384]{1,0:T(8,128)}) %reduce-scatter.15.cloned.1.call-update) | async-done | bytes 1572880 | tf_op jit(solution)/shard_map/reduce_scatter | solution.py:82
  1017.0 28.6 %all-gather.21.cloned.1.call-done = bf16[4096,384]{1,0:T(8,128)(2,1)} async-done(((bf16[1024,384]{1,0:T(8,128)(2,1)}), bf16[4096,384]{1,0:T(8,128)(2,1)}) %all-gather.21.cloned.1.call-update) | async-done | bytes 3145744 | tf_op jit(solution)/shard_map/all_gather | solution.py:65
  1050.5 43.5 %reduce-scatter.21.cloned.1.call-done = f32[2048,192]{0,1:T(8,128)} async-done(((f32[4096,192]{0,1:T(8,128)}), f32[2048,192]{0,1:T(8,128)}) %reduce-scatter.21.cloned.1.call-update) | async-done | bytes 1572880 | tf_op jit(solution)/shard_map/reduce_scatter | solution.py:73
  1096.4 173.6 %while.28 = (s32[]{:T(128)}, f32[1,2048,3,64]{1,3,2,0:T(8,128)}, f32[1,2048,3,64]{1,3,2,0:T(8,128)}, f32[4,1,512,3,64]{2,0,4,3,1:T(4,128)}, s32[4]{0:T(128)S(1)}...) while((s32[]{:T(128)}, f32[1,2048,3,64]{1,3,2,0:T(8,128)}, ...), condition=%wide.region_25.27_spmd.clone, body=%wide.region_23.26_spmd.clone.sunk | while | flops 2063563264 | bytes 151970208 | solution.py:170
  1297.5 42.6 %all-gather.23.cloned.1.call-done = bf16[4096,576]{0,1:T(8,128)(2,1)} async-done(((bf16[2048,576]{0,1:T(8,128)(2,1)}), bf16[4096,576]{0,1:T(8,128)(2,1)}) %all-gather.23.cloned.1.call-update) | async-done | bytes 4718608 | tf_op jit(solution)/shard_map/all_gather | solution.py:69
  1357.9 82.4 %all-reduce.9.cloned.1.call-done = bf16[3,384,768]{2,1,0:T(8,128)(2,1)} async-done(((bf16[3,384,768]{2,1,0:T(8,128)(2,1)}), bf16[3,384,768]{2,1,0:T(8,128)(2,1)}) %all-reduce.9.cloned.1.call-update) | async-done | bytes 1769488 | tf_op jit(solution)/shard_map/psum | solution.py:288
  1443.8 73.8 %all-reduce.11.cloned.1.call-done = (bf16[384,3,192]{0,2,1:T(8,128)(2,1)}, bf16[192,384]{1,0:T(8,128)(2,1)}, bf16[384,768]{1,0:T(8,128)(2,1)}, bf16[384,768]{1,0:T(8,128)(2,1)}) async-done(((bf16[384,3,192]{0,2,1:T(8,128)(2,1)}, bf16[192,384]{1,0:T(8,128)(2,1)}, bf16[384,768]{1,0:T(8,128)(2,1)}, bf16[384,768]{1,0:T(8,128)(2,1)}), (bf16[384,3,192]{0,2,1:T(8,128)(2,1)}, bf16[192,384]{1,0:T(8,128)(2,1)}, ...) | async-done | bytes 1769488 | tf_op jit(solution)/shard_map/psum | solution.py:291
  1524.6 53.3 %reduce-scatter.23.cloned.1.call-done = f32[1024,384]{1,0:T(8,128)} async-done(((f32[4096,384]{1,0:T(8,128)}), f32[1024,384]{1,0:T(8,128)}) %reduce-scatter.23.cloned.1.call-update) | async-done | bytes 1572880 | tf_op jit(solution)/shard_map/reduce_scatter | solution.py:82
  1580.2 32.1 %all-reduce.4 = (bf16[384]{0:T(512)(128)(2,1)S(1)}, bf16[384]{0:T(512)(128)(2,1)S(1)}) all-reduce(bf16[384]{0:T(512)(128)(2,1)S(1)} %get-tuple-element.173, bf16[384]{0:T(512)(128)(2,1)S(1)} %get-tuple-element.178), channel_id=1, replica_groups=mesh['dp'=4,'row'=2,'col'=4] {'dp','col'}, use_global_device_ids=true, to_apply=%region_32.34 | all-reduce | flops 768 | bytes 3072 | tf_op jit(solution)/shard_map/psum | solution.py:286
  (327 shorter events, 415.9 us)
Async XLA Ops:
  7.2 300.2 %copy-start = (bf16[3,384,768]{2,1,0:T(8,128)(2,1)S(1)}, bf16[3,384,768]{2,1,0:T(8,128)(2,1)}, u32[]{:S(2)}) copy-start(bf16[3,384,768]{2,1,0:T(8,128)(2,1)} %param.24) | copy-start | bytes 5308420
  7.2 40.4 %all-gather.9.cloned.1.call-start = ((), (), s32[]{:S(2)}) async-start(), calls=%async_computation.8 | async-start | bytes 3932160 | tf_op jit(solution)/shard_map/all_gather | solution.py:65
  17.2 148.2 %reduce-scatter.9.cloned.1.call-start = ((), (), s32[]{:S(2)}) async-start(), calls=%async_computation.9 | async-start | bytes 14155776 | tf_op jit(solution)/shard_map/reduce_scatter | solution.py:73
  54.7 244.8 %all-gather.11.cloned.1.call-start = ((), (), s32[]{:S(2)}) async-start(), calls=%async_computation.10 | async-start | bytes 2359296 | tf_op jit(solution)/shard_map/all_gather | solution.py:69
  58.9 110.2 %copy-start.18 = (f32[2048,32]{0,1:T(8,128)}, f32[2048,32]{0,1:T(8,128)S(1)}, u32[]{:S(2)}) copy-start(f32[2048,32]{0,1:T(8,128)S(1)} %get-tuple-element.267) | copy-start | bytes 786436
  272.2 91.8 %reduce-scatter.11.cloned.1.call-start = ((), (), s32[]{:S(2)}) async-start(), calls=%async_computation.11 | async-start | bytes 7864320 | tf_op jit(solution)/shard_map/reduce_scatter | solution.py:82
  304.9 89.5 %all-gather.17.cloned.1.call-start = ((), (), s32[]{:S(2)}) async-start(), calls=%async_computation.16 | async-start | bytes 3932160 | tf_op jit(solution)/shard_map/all_gather | solution.py:65
  311.6 113.3 %all-gather.13.cloned.1.call-start = ((), (), s32[]{:S(2)}) async-start(), calls=%async_computation.12 | async-start | bytes 3932160 | tf_op jit(solution)/shard_map/all_gather | solution.py:65
  374.5 197.3 %reduce-scatter.17.cloned.1.call-start = ((), (), s32[]{:S(2)}) async-start(), calls=%async_computation.17 | async-start | bytes 18874368 | tf_op jit(solution)/shard_map/reduce_scatter | solution.py:73
  404.9 313.9 %reduce-scatter.13.cloned.1.call-start = ((), (), s32[]{:S(2)}) async-start(), calls=%async_computation.13 | async-start | bytes 18874368 | tf_op jit(solution)/shard_map/reduce_scatter | solution.py:73
  435.5 372.7 %all-gather.19.cloned.1.call-start = ((), (), s32[]{:S(2)}) async-start(), calls=%async_computation.18 | async-start | bytes 9437184 | tf_op jit(solution)/shard_map/all_gather | solution.py:69
  727.8 162.3 %all-gather.15.cloned.1.call-start = ((), (), s32[]{:S(2)}) async-start(), calls=%async_computation.14 | async-start | bytes 9437184 | tf_op jit(solution)/shard_map/all_gather | solution.py:69
  728.3 223.1 %reduce-scatter.19.cloned.1.call-start = ((), (), s32[]{:S(2)}) async-start(), calls=%async_computation.19 | async-start | bytes 7864320 | tf_op jit(solution)/shard_map/reduce_scatter | solution.py:82
  817.7 195.0 %reduce-scatter.15.cloned.1.call-start = ((), (), s32[]{:S(2)}) async-start(), calls=%async_computation.15 | async-start | bytes 7864320 | tf_op jit(solution)/shard_map/reduce_scatter | solution.py:82
  899.4 146.2 %all-gather.21.cloned.1.call-start = ((), (), s32[]{:S(2)}) async-start(), calls=%async_computation.20 | async-start | bytes 3932160 | tf_op jit(solution)/shard_map/all_gather | solution.py:65
  1016.9 77.1 %reduce-scatter.21.cloned.1.call-start = ((), (), s32[]{:S(2)}) async-start(), calls=%async_computation.21 | async-start | bytes 4718592 | tf_op jit(solution)/shard_map/reduce_scatter | solution.py:73
  1050.4 289.7 %all-gather.23.cloned.1.call-start = ((), (), s32[]{:S(2)}) async-start(), calls=%async_computation.22 | async-start | bytes 7077888 | tf_op jit(solution)/shard_map/all_gather | solution.py:69
  1277.3 162.9 %all-reduce.9.cloned.1.call-start = ((), (), s32[]{:S(2)}) async-start(), calls=%async_computation.24 | async-start | bytes 3538944 | tf_op jit(solution)/shard_map/psum | solution.py:288
  1293.5 224.1 %all-reduce.11.cloned.1.call-start = ((), (), s32[]{:S(2)}) async-start(), calls=%async_computation.25 | async-start | bytes 3538944 | tf_op jit(solution)/shard_map/psum | solution.py:291
  1346.8 231.1 %reduce-scatter.23.cloned.1.call-start = ((), (), s32[]{:S(2)}) async-start(), calls=%async_computation.23 | async-start | bytes 7864320 | tf_op jit(solution)/shard_map/reduce_scatter | solution.py:82
  1443.8 134.1 %copy-start.11 = (bf16[384,1024]{0,1:T(8,128)(2,1)S(1)}, bf16[384,1024]{0,1:T(8,128)(2,1)}, u32[]{:S(2)}) copy-start(bf16[384,1024]{0,1:T(8,128)(2,1)} %copy-done.9) | copy-start | bytes 2359300
  1443.8 134.1 %copy-start.31 = (f32[1024]{0:T(1024)S(1)}, f32[1024]{0:T(1024)}, u32[]{:S(2)}) copy-start(f32[1024]{0:T(1024)} %copy-done.30) | copy-start | bytes 12292
  1443.8 134.1 %copy-start.33 = (f32[1024]{0:T(1024)S(1)}, f32[1024]{0:T(1024)}, u32[]{:S(2)}) copy-start(f32[1024]{0:T(1024)} %copy-done.32) | copy-start | bytes 12292
  1443.8 134.1 %copy-start.35 = (f32[384]{0:T(512)S(1)}, f32[384]{0:T(512)}, u32[]{:S(2)}) copy-start(f32[384]{0:T(512)} %param.18) | copy-start | bytes 4612
  (64 other events, 860.2 us)
Sparse Core Ops, SparseCore 0:
  17.3 30.2 all-gather.8
  54.8 110.6 reduce-scatter.8
  272.3 27.1 all-gather.10
  305.0 58.8 reduce-scatter.10
  365.9 28.4 all-gather.16
  396.4 28.4 all-gather.12
  427.3 144.5 reduce-scatter.16
  574.1 144.5 reduce-scatter.12
  727.9 80.3 all-gather.18
  809.6 80.3 all-gather.14
  892.6 58.8 reduce-scatter.18
  953.8 58.8 reduce-scatter.14
  1017.1 28.5 all-gather.20
  1050.6 43.3 reduce-scatter.20
  1277.4 62.6 all-gather.22
  1343.5 96.7 all-reduce.8
  1443.3 74.3 all-reduce.10
  1520.0 57.8 reduce-scatter.22
where the time goes:
time: 1640 us; the launch traced here: 1630 us
  waiting for transfers between devices  1120 us (68%)
  matrix products  243 us (15%)
  other arithmetic  111 us (7%)
  local copies, waits for them, and re-layouts  68.2 us (4%)
  blocking collectives  53.1 us (3%)
  between operations  16.6 us (1%)
  loops' own time  16.4 us (1%)
    reduce_scatter x4, waiting for transfers between devices, row_product(): lax.psum_scatter(jnp.dot(gathered, tile_part, preferred_element_type=jnp....  433 us
    all_gather x4, waiting for transfers between devices, gather_rows(): return lax.all_gather(local_part, 'row', axis=0, tiled=True)  222 us
    reduce_scatter x4, waiting for transfers between devices, col_product(): lax.psum_scatter(jnp.dot(gathered, tile_part, preferred_element_type=jnp....  211 us
    all_gather x4, waiting for transfers between devices, gather_col(): return lax.all_gather(local_part, 'col', axis=0, tiled=True)  98.9 us
    psum x1, waiting for transfers between devices, local(): lax.psum(mod_part.astype(jnp.bfloat16), ('dp', 'col')).astype(jnp.float32)  82.4 us
    psum x1, waiting for transfers between devices, local(): lax.psum(qkv_grad.astype(jnp.bfloat16), 'dp').astype(jnp.float32)  73.8 us
    dot_general x8, matrix products, masked_scores(): jnp.einsum('sqhd,skhd->shqk', query_part, key_rows, preferred_element_typ...  40.6 us
    dynamic_update_slice x8, local copies, waits for them, and re-layouts, attend_forward(): block_outs, log_totals = lax.map(one_block, offsets)  36.1 us
  transfers between devices with their start and end apart: 18, of which 18 were waited for; matrix products, arithmetic and copies ran while one was open for 6% of the time, Pallas kernels for 0%

commit v1 on v0

--- a/solution.py
+++ b/solution.py
@@ -11,6 +11,28 @@
 HIGH = lax.Precision.HIGHEST
 
 
+def joined_along(pieces, dim):
+    pieces = jnp.moveaxis(pieces, 0, dim)
+    shape = pieces.shape
+    return pieces.reshape(*shape[:dim], shape[dim] * shape[dim + 1], *shape[dim + 2 :])
+
+
+def collect(array, axis, dim):
+    length = lax.axis_size(axis)
+    pairs = [(i, (i + 1) % length) for i in range(length)]
+    back = [(b, a) for a, b in pairs]
+    lower, upper = ([], [])
+    for step in range(length - 1):
+        if step % 2 == 0:
+            lower.append(lax.ppermute(lower[-1] if lower else array, axis, pairs))
+        else:
+            upper.append(lax.ppermute(upper[-1] if upper else array, axis, back))
+    blocks = jnp.stack([*lower[::-1], array, *upper])
+    shift = lax.axis_index(axis) - len(lower)
+    blocks = blocks[(jnp.arange(length) - shift) % length]
+    return joined_along(blocks, dim)
+
+
 def time_embed(steps_in, width_all):
     half_width = width_all // 2
     frequency = jnp.exp(-math.log(10000.0) * jnp.arange(half_width, dtype=jnp.float32) / half_width)
@@ -62,7 +84,7 @@
 
 
 def gather_col(local_part):
-    return lax.all_gather(local_part, "col", axis=0, tiled=True)
+    return collect(local_part, "col", 0)
 
 
 def gather_rows(local_part):

time: 1640 us -> 1610 us (0.982)
  waiting for transfers between devices: 1120 us -> 1050 us
  local copies, waits for them, and re-layouts: 68.2 us -> 86.7 us
    ppermute x0 -> x12, waiting for transfers between devices: none -> 120 us  [the longest x8 118 us: collect(): lower.append(lax.ppermute(lower[-1] if lower else array, axis, pairs))]
    all_gather x4 -> x0, waiting for transfers between devices: 98.9 us -> none  [gather_col(): return lax.all_gather(local_part, 'col', axis=0, tiled=True)]
    reduce_scatter x4, waiting for transfers between devices: 211 us -> 159 us  [col_product(): lax.psum_scatter(jnp.dot(gathered, tile_part, preferred_element_type=jnp....]
    reduce_scatter x4, waiting for transfers between devices: 433 us -> 390 us  [row_product(): lax.psum_scatter(jnp.dot(gathered, tile_part, preferred_element_type=jnp....]
    gather x0 -> x4, local copies, waits for them, and re-layouts: none -> 18.8 us  [collect(): blocks = blocks[(jnp.arange(length) - shift) % length]]
  transfers between devices with their start and end apart: 18 -> 26, of which waited for: 18 -> 22; matrix products, arithmetic and copies ran while one was open for 6% -> 7% of each run, Pallas kernels for 0% -> 0%
where the time goes in v1:
time: 1610 us; the launch traced here: 1600 us
  waiting for transfers between devices  1050 us (65%)
  matrix products  242 us (15%)
  other arithmetic  119 us (7%)
  local copies, waits for them, and re-layouts  86.7 us (5%)
  blocking collectives  53.1 us (3%)
  starting transfers between devices  17 us (1%)
  loops' own time  16.4 us (1%)
  between operations  16.1 us (1%)
    reduce_scatter x4, waiting for transfers between devices, row_product(): lax.psum_scatter(jnp.dot(gathered, tile_part, preferred_element_type=jnp....  390 us
    all_gather x4, waiting for transfers between devices, gather_rows(): return lax.all_gather(local_part, 'row', axis=0, tiled=True)  222 us
    reduce_scatter x4, waiting for transfers between devices, col_product(): lax.psum_scatter(jnp.dot(gathered, tile_part, preferred_element_type=jnp....  159 us
    ppermute x8, waiting for transfers between devices, collect(): lower.append(lax.ppermute(lower[-1] if lower else array, axis, pairs))  118 us
    psum x1, waiting for transfers between devices, local(): lax.psum(mod_part.astype(jnp.bfloat16), ('dp', 'col')).astype(jnp.float32)  82.2 us
    psum x1, waiting for transfers between devices, local(): lax.psum(qkv_grad.astype(jnp.bfloat16), 'dp').astype(jnp.float32)  74 us
    dot_general x8, matrix products, masked_scores(): jnp.einsum('sqhd,skhd->shqk', query_part, key_rows, preferred_element_typ...  40.7 us
    dynamic_update_slice x8, local copies, waits for them, and re-layouts, attend_forward(): block_outs, log_totals = lax.map(one_block, offsets)  36 us
  transfers between devices with their start and end apart: 26, of which 22 were waited for; matrix products, arithmetic and copies ran while one was open for 7% of the time, Pallas kernels for 0%

profile of v1, /device:TPU:0, one launch (start us, length us, event | category | flops | bytes accessed | tf_op | source)
XLA Modules:
  0.0 1599.7 jit_solution(3709685258352076811)
XLA Ops:
  18.3 16.0 collective-permute-done
  64.6 109.9 %reduce-scatter.9.cloned.1.call-done = f32[2048,576]{0,1:T(8,128)} async-done(((f32[4096,576]{0,1:T(8,128)}), f32[2048,576]{0,1:T(8,128)}) %reduce-scatter.9.cloned.1.call-update) | async-done | bytes 4718608 | tf_op jit(solution)/shard_map/reduce_scatter | solution.py:95
  179.6 98.8 %while.27 = (s32[]{:T(128)}, bf16[4,1,512,3,64]{2,4,3,1,0:T(8,128)(2,1)}, f32[4,1,3,512]{3,2,1,0:T(4,128)S(1)}, s32[1,2048]{1,0:T(1,128)S(1)}, s32[4]{0:T(128)S(...) while((s32[]{:T(128)}, ...), condition=%wide.region_8.10_spmd, body=%wide.region_5.9_spmd.sunk | while | flops 844102144 | bytes 50471144 | solution.py:146
  281.3 27.3 %all-gather.5.cloned.1.call-done = bf16[4096,192]{0,1:T(8,128)(2,1)} async-done(((bf16[2048,192]{0,1:T(8,128)(2,1)}), bf16[4096,192]{0,1:T(8,128)(2,1)}) %all-gather.5.cloned.1.call-update) | async-done | bytes 1572880 | tf_op jit(solution)/shard_map/all_gather | solution.py:91
  321.5 17.4 %collective-permute-done.6 = bf16[1024,384]{1,0:T(8,128)(2,1)S(1)} collective-permute-done((bf16[1024,384]{1,0:T(8,128)(2,1)S(1)}, bf16[1024,384]{1,0:T(8,128)(2,1)S(1)}, u32[]{:S(2)}, u32[]{:S(2)}) %collective-permute-start.6) | collective-permute-done | bytes 786464 | tf_op jit(solution)/shard_map/ppermute | solution.py:27
  343.4 24.6 %collective-permute-done.7 = bf16[1024,384]{1,0:T(8,128)(2,1)S(1)} collective-permute-done((bf16[1024,384]{1,0:T(8,128)(2,1)S(1)}, bf16[1024,384]{1,0:T(8,128)(2,1)S(1)}, u32[]{:S(2)}, u32[]{:S(2)}) %collective-permute-start.7) | collective-permute-done | bytes 786464 | tf_op jit(solution)/shard_map/ppermute | solution.py:27
  374.7 9.9 fusion.91
  397.3 14.1 collective-permute-done.3
  430.5 10.1 fusion.89
  441.1 90.4 %reduce-scatter.17.cloned.1.call-done = f32[2048,768]{1,0:T(8,128)} async-done(((f32[4096,768]{1,0:T(8,128)}), f32[2048,768]{1,0:T(8,128)}) %reduce-scatter.17.cloned.1.call-update) | async-done | bytes 6291472 | tf_op jit(solution)/shard_map/reduce_scatter | solution.py:95
  531.4 146.8 %reduce-scatter.13.cloned.1.call-done = f32[2048,768]{1,0:T(8,128)} async-done(((f32[4096,768]{1,0:T(8,128)}), f32[2048,768]{1,0:T(8,128)}) %reduce-scatter.13.cloned.1.call-update) | async-done | bytes 6291472 | tf_op jit(solution)/shard_map/reduce_scatter | solution.py:95
  688.1 79.7 %all-gather.9.cloned.1.call-done = bf16[4096,768]{1,0:T(8,128)(2,1)} async-done(((bf16[2048,768]{1,0:T(8,128)(2,1)}), bf16[4096,768]{1,0:T(8,128)(2,1)}) %all-gather.9.cloned.1.call-update) | async-done | bytes 6291472 | tf_op jit(solution)/shard_map/all_gather | solution.py:91
  777.4 72.3 %all-gather.7.cloned.1.call-done = bf16[4096,768]{1,0:T(8,128)(2,1)} async-done(((bf16[2048,768]{1,0:T(8,128)(2,1)}), bf16[4096,768]{1,0:T(8,128)(2,1)}) %all-gather.7.cloned.1.call-update) | async-done | bytes 6291472 | tf_op jit(solution)/shard_map/all_gather | solution.py:91
  859.3 51.9 %reduce-scatter.19.cloned.1.call-done = f32[1024,384]{1,0:T(8,128)} async-done(((f32[4096,384]{1,0:T(8,128)}), f32[1024,384]{1,0:T(8,128)}) %reduce-scatter.19.cloned.1.call-update) | async-done | bytes 1572880 | tf_op jit(solution)/shard_map/reduce_scatter | solution.py:104
  918.8 53.7 %reduce-scatter.15.cloned.1.call-done = f32[1024,384]{1,0:T(8,128)} async-done(((f32[4096,384]{1,0:T(8,128)}), f32[1024,384]{1,0:T(8,128)}) %reduce-scatter.15.cloned.1.call-update) | async-done | bytes 1572880 | tf_op jit(solution)/shard_map/reduce_scatter | solution.py:104
  978.4 17.4 %collective-permute-done.9 = bf16[1024,384]{1,0:T(8,128)(2,1)S(1)} collective-permute-done((bf16[1024,384]{1,0:T(8,128)(2,1)S(1)}, bf16[1024,384]{1,0:T(8,128)(2,1)S(1)}, u32[]{:S(2)}, u32[]{:S(2)}) %collective-permute-start.9) | collective-permute-done | bytes 786464 | tf_op jit(solution)/shard_map/ppermute | solution.py:27
  995.8 11.4 collective-permute-done.10
  1018.7 43.3 %reduce-scatter.21.cloned.1.call-done = f32[2048,192]{0,1:T(8,128)} async-done(((f32[4096,192]{0,1:T(8,128)}), f32[2048,192]{0,1:T(8,128)}) %reduce-scatter.21.cloned.1.call-update) | async-done | bytes 1572880 | tf_op jit(solution)/shard_map/reduce_scatter | solution.py:95
  1064.4 173.7 %while.28 = (s32[]{:T(128)}, f32[1,2048,3,64]{1,3,2,0:T(8,128)}, f32[1,2048,3,64]{1,3,2,0:T(8,128)}, f32[4,1,512,3,64]{2,0,4,3,1:T(4,128)}, s32[4]{0:T(128)S(1)}...) while((s32[]{:T(128)}, f32[1,2048,3,64]{1,3,2,0:T(8,128)}, ...), condition=%wide.region_25.27_spmd.clone, body=%wide.region_23.26_spmd.clone.sunk | while | flops 2063563264 | bytes 151970208 | solution.py:192
  1265.6 42.6 %all-gather.11.cloned.1.call-done = bf16[4096,576]{0,1:T(8,128)(2,1)} async-done(((bf16[2048,576]{0,1:T(8,128)(2,1)}), bf16[4096,576]{0,1:T(8,128)(2,1)}) %all-gather.11.cloned.1.call-update) | async-done | bytes 4718608 | tf_op jit(solution)/shard_map/all_gather | solution.py:91
  1326.0 82.2 %all-reduce.9.cloned.1.call-done = bf16[3,384,768]{2,1,0:T(8,128)(2,1)} async-done(((bf16[3,384,768]{2,1,0:T(8,128)(2,1)}), bf16[3,384,768]{2,1,0:T(8,128)(2,1)}) %all-reduce.9.cloned.1.call-update) | async-done | bytes 1769488 | tf_op jit(solution)/shard_map/psum | solution.py:310
  1411.8 74.0 %all-reduce.11.cloned.1.call-done = (bf16[384,3,192]{0,2,1:T(8,128)(2,1)}, bf16[192,384]{1,0:T(8,128)(2,1)}, bf16[384,768]{1,0:T(8,128)(2,1)}, bf16[384,768]{1,0:T(8,128)(2,1)}) async-done(((bf16[384,3,192]{0,2,1:T(8,128)(2,1)}, bf16[192,384]{1,0:T(8,128)(2,1)}, bf16[384,768]{1,0:T(8,128)(2,1)}, bf16[384,768]{1,0:T(8,128)(2,1)}), (bf16[384,3,192]{0,2,1:T(8,128)(2,1)}, bf16[192,384]{1,0:T(8,128)(2,1)}, ...) | async-done | bytes 1769488 | tf_op jit(solution)/shard_map/psum | solution.py:313
  1492.7 53.3 %reduce-scatter.23.cloned.1.call-done = f32[1024,384]{1,0:T(8,128)} async-done(((f32[4096,384]{1,0:T(8,128)}), f32[1024,384]{1,0:T(8,128)}) %reduce-scatter.23.cloned.1.call-update) | async-done | bytes 1572880 | tf_op jit(solution)/shard_map/reduce_scatter | solution.py:104
  1548.3 32.1 %all-reduce.4 = (bf16[384]{0:T(512)(128)(2,1)S(1)}, bf16[384]{0:T(512)(128)(2,1)S(1)}) all-reduce(bf16[384]{0:T(512)(128)(2,1)S(1)} %get-tuple-element.173, bf16[384]{0:T(512)(128)(2,1)S(1)} %get-tuple-element.178), channel_id=1, replica_groups=mesh['dp'=4,'row'=2,'col'=4] {'dp','col'}, use_global_device_ids=true, to_apply=%region_32.34 | all-reduce | flops 768 | bytes 3072 | tf_op jit(solution)/shard_map/psum | solution.py:308
  (350 shorter events, 486.8 us)
Async XLA Ops:
  7.2 167.3 %reduce-scatter.9.cloned.1.call-start = ((), (), s32[]{:S(2)}) async-start(), calls=%async_computation.8 | async-start | bytes 14155776 | tf_op jit(solution)/shard_map/reduce_scatter | solution.py:95
  16.6 17.7 %collective-permute-start = (bf16[1024,384]{1,0:T(8,128)(2,1)}, bf16[1024,384]{1,0:T(8,128)(2,1)S(1)}, u32[]{:S(2)}, u32[]{:S(2)}) collective-permute-start(bf16[1024,384]{1,0:T(8,128)(2,1)} %fusion.61), channel_id=1, source_target_pairs={{0,1},{1,2},{2,3},{3,0},{4,5},{5,6},{6,7},{7,4},{8,9},{9,10},{10,1... | collective-permute-start | bytes 2359304 | tf_op jit(solution)/shard_map/ppermute | solution.py:27
  16.6 20.0 %collective-permute-start.2 = (bf16[1024,384]{1,0:T(8,128)(2,1)}, bf16[1024,384]{1,0:T(8,128)(2,1)}, u32[]{:S(2)}, u32[]{:S(2)}) collective-permute-start(bf16[1024,384]{1,0:T(8,128)(2,1)} %fusion.61), channel_id=1, source_target_pairs={{1,0},{2,1},{3,2},{0,3},{5,4},{6,5},{7,6},{4,7},{9,8},{10,9},{11,1... | collective-permute-start | bytes 2359304 | tf_op jit(solution)/shard_map/ppermute | solution.py:29
  60.4 248.2 %all-gather.5.cloned.1.call-start = ((), (), s32[]{:S(2)}) async-start(), calls=%async_computation.9 | async-start | bytes 2359296 | tf_op jit(solution)/shard_map/all_gather | solution.py:91
  281.3 103.4 %reduce-scatter.11.cloned.1.call-start = ((), (), s32[]{:S(2)}) async-start(), calls=%async_computation.10 | async-start | bytes 7864320 | tf_op jit(solution)/shard_map/reduce_scatter | solution.py:104
  313.9 217.5 %reduce-scatter.17.cloned.1.call-start = ((), (), s32[]{:S(2)}) async-start(), calls=%async_computation.14 | async-start | bytes 18874368 | tf_op jit(solution)/shard_map/reduce_scatter | solution.py:95
  319.7 19.2 %collective-permute-start.6 = (bf16[1024,384]{1,0:T(8,128)(2,1)S(1)}, bf16[1024,384]{1,0:T(8,128)(2,1)S(1)}, u32[]{:S(2)}, u32[]{:S(2)}) collective-permute-start(bf16[1024,384]{1,0:T(8,128)(2,1)S(1)} %fusion.69), channel_id=1, source_target_pairs={{0,1},{1,2},{2,3},{3,0},{4,5},{5,6},{6,7},{7,4},{8,9},{9,10},{10,1... | collective-permute-start | bytes 2359304 | tf_op jit(solution)/shard_map/ppermute | solution.py:27
  319.7 23.7 %collective-permute-start.8 = (bf16[1024,384]{1,0:T(8,128)(2,1)S(1)}, bf16[1024,384]{1,0:T(8,128)(2,1)S(1)}, u32[]{:S(2)}, u32[]{:S(2)}) collective-permute-start(bf16[1024,384]{1,0:T(8,128)(2,1)S(1)} %fusion.69), channel_id=1, source_target_pairs={{1,0},{2,1},{3,2},{0,3},{5,4},{6,5},{7,6},{4,7},{9,8},{10,9},{11,1... | collective-permute-start | bytes 2359304 | tf_op jit(solution)/shard_map/ppermute | solution.py:29
  338.8 29.1 %collective-permute-start.7 = (bf16[1024,384]{1,0:T(8,128)(2,1)S(1)}, bf16[1024,384]{1,0:T(8,128)(2,1)S(1)}, u32[]{:S(2)}, u32[]{:S(2)}) collective-permute-start(bf16[1024,384]{1,0:T(8,128)(2,1)S(1)} %collective-permute-done.6), channel_id=1, source_target_pairs={{0,1},{1,2},{2,3},{3,0},{4,5},{5,6},{6,7},{7,4},{8,9},{9,10},{10,1... | collective-permute-start | bytes 2359304 | tf_op jit(solution)/shard_map/ppermute | solution.py:27
  384.6 293.7 %reduce-scatter.13.cloned.1.call-start = ((), (), s32[]{:S(2)}) async-start(), calls=%async_computation.11 | async-start | bytes 18874368 | tf_op jit(solution)/shard_map/reduce_scatter | solution.py:95
  395.5 15.9 collective-permute-start.3
  395.9 19.8 %collective-permute-start.5 = (bf16[1024,384]{1,0:T(8,128)(2,1)S(1)}, bf16[1024,384]{1,0:T(8,128)(2,1)S(1)}, u32[]{:S(2)}, u32[]{:S(2)}) collective-permute-start(bf16[1024,384]{1,0:T(8,128)(2,1)S(1)} %add_convert_fusion.1), channel_id=1, source_target_pairs={{1,0},{2,1},{3,2},{0,3},{5,4},{6,5},{7,6},{4,7},{9,8},{10,9},{11,1... | collective-permute-start | bytes 2359304 | tf_op jit(solution)/shard_map/ppermute | solution.py:29
  411.4 12.4 collective-permute-start.4
  440.6 327.2 %all-gather.9.cloned.1.call-start = ((), (), s32[]{:S(2)}) async-start(), calls=%async_computation.15 | async-start | bytes 9437184 | tf_op jit(solution)/shard_map/all_gather | solution.py:91
  687.3 162.4 %all-gather.7.cloned.1.call-start = ((), (), s32[]{:S(2)}) async-start(), calls=%async_computation.12 | async-start | bytes 9437184 | tf_op jit(solution)/shard_map/all_gather | solution.py:91
  688.0 223.1 %reduce-scatter.19.cloned.1.call-start = ((), (), s32[]{:S(2)}) async-start(), calls=%async_computation.16 | async-start | bytes 7864320 | tf_op jit(solution)/shard_map/reduce_scatter | solution.py:104
  777.3 195.2 %reduce-scatter.15.cloned.1.call-start = ((), (), s32[]{:S(2)}) async-start(), calls=%async_computation.13 | async-start | bytes 7864320 | tf_op jit(solution)/shard_map/reduce_scatter | solution.py:104
  859.2 202.8 %reduce-scatter.21.cloned.1.call-start = ((), (), s32[]{:S(2)}) async-start(), calls=%async_computation.17 | async-start | bytes 4718592 | tf_op jit(solution)/shard_map/reduce_scatter | solution.py:95
  976.6 19.2 %collective-permute-start.9 = (bf16[1024,384]{1,0:T(8,128)(2,1)S(1)}, bf16[1024,384]{1,0:T(8,128)(2,1)S(1)}, u32[]{:S(2)}, u32[]{:S(2)}) collective-permute-start(bf16[1024,384]{1,0:T(8,128)(2,1)S(1)} %get-tuple-element.257), channel_id=1, source_target_pairs={{0,1},{1,2},{2,3},{3,0},{4,5},{5,6},{6,7},{7,4},{8,9},{9,10},{10,1... | collective-permute-start | bytes 2359304 | tf_op jit(solution)/shard_map/ppermute | solution.py:27
  976.6 19.2 %collective-permute-start.11 = (bf16[1024,384]{1,0:T(8,128)(2,1)S(1)}, bf16[1024,384]{1,0:T(8,128)(2,1)S(1)}, u32[]{:S(2)}, u32[]{:S(2)}) collective-permute-start(bf16[1024,384]{1,0:T(8,128)(2,1)S(1)} %get-tuple-element.257), channel_id=1, source_target_pairs={{1,0},{2,1},{3,2},{0,3},{5,4},{6,5},{7,6},{4,7},{9,8},{10,9},{11,1... | collective-permute-start | bytes 2359304 | tf_op jit(solution)/shard_map/ppermute | solution.py:29
  1018.6 289.6 %all-gather.11.cloned.1.call-start = ((), (), s32[]{:S(2)}) async-start(), calls=%async_computation.18 | async-start | bytes 7077888 | tf_op jit(solution)/shard_map/all_gather | solution.py:91
  1245.5 162.7 %all-reduce.9.cloned.1.call-start = ((), (), s32[]{:S(2)}) async-start(), calls=%async_computation.20 | async-start | bytes 3538944 | tf_op jit(solution)/shard_map/psum | solution.py:310
  1261.7 224.1 %all-reduce.11.cloned.1.call-start = ((), (), s32[]{:S(2)}) async-start(), calls=%async_computation.21 | async-start | bytes 3538944 | tf_op jit(solution)/shard_map/psum | solution.py:313
  1315.0 231.0 %reduce-scatter.23.cloned.1.call-start = ((), (), s32[]{:S(2)}) async-start(), calls=%async_computation.19 | async-start | bytes 7864320 | tf_op jit(solution)/shard_map/reduce_scatter | solution.py:104
  (71 other events, 1639.0 us)
Sparse Core Ops, SparseCore 0:
  60.5 113.9 reduce-scatter.8
  281.4 27.1 all-gather.4
  314.1 69.3 reduce-scatter.10
  385.7 145.7 reduce-scatter.16
  533.6 144.6 reduce-scatter.12
  687.4 80.3 all-gather.8
  769.3 80.3 all-gather.6
  852.2 58.8 reduce-scatter.18
  913.7 58.8 reduce-scatter.14
  1018.7 43.2 reduce-scatter.20
  1245.6 62.6 all-gather.10
  1311.6 96.5 all-reduce.8
  1411.4 74.2 all-reduce.10
  1488.1 57.8 reduce-scatter.22
